TPU v7x, 32 devices: a whole 2x2x4 slice. The times are simulated.
32 devices in a mesh: grp: 2 (over x), seq: 8 (over z, y), mdl: 2 (over core).
Axes of the slice: x: 2, y: 2, z: 4, core: 2. Of those that a mesh axis runs over, the one named last changes fastest.
Arguments:
- signal: float32 [8, 128, 8192], P('grp', 'mdl', 'seq'), parts along dimension 0, may hold values from -6 to 6
- lengths: int32 [8], P('grp'), parts along dimension 0, may hold values from 1 to 64, 160 in all
- chan_weight: bfloat16 [128, 128, 16], P('mdl'), may hold values from -0.5 to 0.5
- up_weight: bfloat16 [4, 2048, 4096], P(None, 'seq', 'mdl'), may hold values from -0.125 to 0.125
- down_weight: bfloat16 [4, 2048, 4096], P(None, 'seq', 'mdl'), may hold values from -0.09375 to 0.09375
Outputs:
- features: bfloat16 [8, 64, 2048], P(('grp', 'mdl'), 'seq'), parts along dimension 0
There are 2 independent parts, one for each index of `grp`. A program takes and returns all parts, laid end to end along the dimension named above; an argument that names none is the same for every part. Nothing has to cross between parts.
Inputs may be any that keep to these rules, and one draw needn't show every extreme that they name: `lengths`: live windows of each recording; one recording is live for all 64, and all recordings together have (320) // 2.
All inputs are finite; a program needn't handle non-finite values.
Results may differ from a plain program's by a relative error of at most 0.014.
Values may be sent and summed in bfloat16 or wider, within the bound.
A program may use at most 128 MiB of HBM per device.

v0:
```python
import math
import jax
import jax.numpy as jnp
from jax import lax
from jax.sharding import PartitionSpec as P

HOP = 128
EPSILON = 1e-06


def shifted(x, axis, by):
    size = lax.axis_size(axis)
    pairs = [(i, i + by) for i in range(size) if 0 <= i + by < size]
    return lax.ppermute(x, axis, pairs)


def spectral_table(half_span):
    full_span = 2 * half_span
    row_index = jnp.arange(full_span, dtype=jnp.int32)
    col_index = jnp.arange(half_span, dtype=jnp.int32)
    phases = row_index[:, None] * col_index[None, :] % full_span
    angles = phases.astype(jnp.float32) * (2.0 * math.pi / full_span)
    window_taper = 0.5 - 0.5 * jnp.cos(row_index.astype(jnp.float32) * (2.0 * math.pi / full_span))
    weighting = window_taper * (1.0 / math.sqrt(full_span))
    joined = jnp.concatenate([jnp.cos(angles), -jnp.sin(angles)], axis=1) * weighting[:, None]
    return jnp.concatenate([joined[:half_span], joined[half_span:]], axis=1)


def log_power(spectrum):
    half_span = spectrum.shape[-1] // 2
    real_part = spectrum[..., :half_span]
    imag_part = spectrum[..., half_span:]
    return jnp.log1p(real_part * real_part + imag_part * imag_part).astype(jnp.bfloat16)


def project_down(hidden, own_down):
    return lax.dot_general(
        hidden, own_down, (((1,), (1,)), ((), ())), preferred_element_type=jnp.float32
    )


def apply_layer(state, up_rows, down_rows, width):
    values = state.astype(jnp.float32)
    squares = lax.psum(jnp.sum(values * values, axis=1, keepdims=True), "seq")
    partial = jnp.dot(state, up_rows, preferred_element_type=jnp.float32).astype(jnp.bfloat16)
    summed = lax.psum_scatter(partial, "seq", scatter_dimension=1, tiled=True)
    scale = lax.rsqrt(squares * (1.0 / width) + EPSILON)
    hidden = jax.nn.gelu(summed.astype(jnp.float32) * scale).astype(jnp.bfloat16)
    hidden = lax.all_gather(hidden, "seq", axis=1, tiled=True)
    added = lax.psum(project_down(hidden, down_rows), "mdl")
    return (values + added).astype(jnp.bfloat16)


def body(signal, lengths, chan_weight, up_weight, down_weight):
    streams, channels, samples = signal.shape
    frames = samples // HOP
    dft_table = spectral_table(HOP)
    boundary = shifted(signal[:, :, :HOP], "seq", -1)
    local_part = jnp.dot(
        signal.reshape(streams, channels, frames, HOP), dft_table, precision=lax.Precision.HIGHEST
    )
    edge_part = jnp.dot(boundary, dft_table[:, 2 * HOP :], precision=lax.Precision.HIGHEST)
    following = jnp.concatenate([local_part[:, :, 1:, 2 * HOP :], edge_part[:, :, None, :]], axis=2)
    spectrum = local_part[..., : 2 * HOP] + following
    logpower = log_power(spectrum)
    embedded = jnp.einsum(
        "scfb,cbe->sfce", logpower, chan_weight, preferred_element_type=jnp.float32
    )
    embedded = embedded.reshape(streams, frames, channels * chan_weight.shape[2])
    frame_index = lax.axis_index("seq") * frames + jnp.arange(frames, dtype=jnp.int32)
    live_mask = frame_index[None, :] < lengths[:, None]
    tokens = jnp.where(live_mask[:, :, None], embedded, 0.0).astype(jnp.bfloat16)
    rows = lax.all_gather(tokens.reshape(streams * frames, -1), "mdl", axis=1, tiled=True)
    state = lax.all_to_all(rows, "seq", split_axis=1, concat_axis=0, tiled=True)
    width = rows.shape[1]
    for layer in range(up_weight.shape[0]):
        state = apply_layer(state, up_weight[layer], down_weight[layer], width)
    rows = lax.all_to_all(state, "seq", split_axis=0, concat_axis=1, tiled=True)
    full_rows = rows.reshape(streams, frames, width)
    half_streams = streams // lax.axis_size("mdl")
    return lax.dynamic_slice_in_dim(
        full_rows, lax.axis_index("mdl") * half_streams, half_streams, 0
    )


def solution(mesh):
    return jax.shard_map(
        body,
        mesh=mesh,
        in_specs=(
            P("grp", "mdl", "seq"),
            P("grp"),
            P("mdl", None, None),
            P(None, "seq", "mdl"),
            P(None, "seq", "mdl"),
        ),
        out_specs=P(("grp", "mdl"), "seq", None),
        check_vma=False,
    )
```

profile of v0, /device:TPU:0, one launch (start us, length us, event | category | flops | bytes accessed | tf_op | source)
XLA Modules:
  0.0 576.4 jit_solution(18243975974515709880)
XLA Ops:
  9.5 4.7 convolution_bitcast_fusion
  22.9 15.4 %all_to_all.35 = bf16[32,8,256]{2,0,1:T(8,128)(2,1)S(1)} all-to-all(bf16[32,8,256]{2,0,1:T(8,128)(2,1)S(1)} %bitcast.87), channel_id=1, replica_groups=mesh['grp'=2,'seq'=8,'mdl'=2] {'seq'}, dimensions={1} | all-to-all | bytes 262144 | tf_op jit(solution)/shard_map/all_to_all | solution.py:74
  41.3 18.6 %psum.56 = f32[256,1]{0,1:T(1,128)S(1)} all-reduce(f32[256,1]{0,1:T(1,128)S(1)} %broadcast_in_dim.36), channel_id=1, replica_groups=mesh['grp'=2,'seq'=8,'mdl'=2] {'seq'}, use_global_device_ids=true, to_apply=%region_2.3 | all-reduce | flops 256 | bytes 2048 | tf_op jit(solution)/shard_map/psum | solution.py:44
  59.9 43.4 %reduce-scatter.5.cloned.1.call-done = bf16[256,256]{1,0:T(8,128)(2,1)} async-done(((bf16[256,2048]{1,0:T(8,128)(2,1)}), bf16[256,256]{1,0:T(8,128)(2,1)}) %reduce-scatter.5.cloned.1.call-update) | async-done | bytes 131088 | tf_op jit(solution)/shard_map/reduce_scatter | solution.py:46
  105.0 39.1 %all-gather.5.cloned.1.call-done = bf16[256,2048]{1,0:T(8,128)(2,1)} async-done(((bf16[256,256]{1,0:T(8,128)(2,1)}), bf16[256,2048]{1,0:T(8,128)(2,1)}) %all-gather.5.cloned.1.call-update) | async-done | bytes 1048592 | tf_op jit(solution)/shard_map/all_gather | solution.py:49
  144.1 2.7 fusion.14
  146.9 17.3 %all-reduce.5.cloned.1.call-done = f32[256,256]{1,0:T(8,128)} async-done(((f32[256,256]{1,0:T(8,128)}), f32[256,256]{1,0:T(8,128)}) %all-reduce.5.cloned.1.call-update) | async-done | bytes 262160 | tf_op jit(solution)/shard_map/psum | solution.py:50
  168.0 21.7 %psum.58 = f32[256,1]{0,1:T(1,128)S(1)} all-reduce(f32[256,1]{0,1:T(1,128)S(1)} %bitcast.88), channel_id=1, replica_groups=mesh['grp'=2,'seq'=8,'mdl'=2] {'seq'}, use_global_device_ids=true, to_apply=%region_6.7 | all-reduce | flops 256 | bytes 2048 | tf_op jit(solution)/shard_map/psum | solution.py:44
  189.7 43.6 %reduce-scatter.7.cloned.1.call-done = bf16[256,256]{1,0:T(8,128)(2,1)} async-done(((bf16[256,2048]{1,0:T(8,128)(2,1)}), bf16[256,256]{1,0:T(8,128)(2,1)}) %reduce-scatter.7.cloned.1.call-update) | async-done | bytes 131088 | tf_op jit(solution)/shard_map/reduce_scatter | solution.py:46
  235.1 38.8 %all-gather.7.cloned.1.call-done = bf16[256,2048]{1,0:T(8,128)(2,1)} async-done(((bf16[256,256]{1,0:T(8,128)(2,1)}), bf16[256,2048]{1,0:T(8,128)(2,1)}) %all-gather.7.cloned.1.call-update) | async-done | bytes 1048592 | tf_op jit(solution)/shard_map/all_gather | solution.py:49
  273.9 2.7 fusion.11
  276.7 17.3 %all-reduce.7.cloned.1.call-done = f32[256,256]{1,0:T(8,128)} async-done(((f32[256,256]{1,0:T(8,128)}), f32[256,256]{1,0:T(8,128)}) %all-reduce.7.cloned.1.call-update) | async-done | bytes 262160 | tf_op jit(solution)/shard_map/psum | solution.py:50
  297.8 21.7 %psum.60 = f32[256,1]{0,1:T(1,128)S(1)} all-reduce(f32[256,1]{0,1:T(1,128)S(1)} %bitcast.89), channel_id=1, replica_groups=mesh['grp'=2,'seq'=8,'mdl'=2] {'seq'}, use_global_device_ids=true, to_apply=%region_10.11 | all-reduce | flops 256 | bytes 2048 | tf_op jit(solution)/shard_map/psum | solution.py:44
  319.5 43.6 %reduce-scatter.9.cloned.1.call-done = bf16[256,256]{1,0:T(8,128)(2,1)} async-done(((bf16[256,2048]{1,0:T(8,128)(2,1)}), bf16[256,256]{1,0:T(8,128)(2,1)}) %reduce-scatter.9.cloned.1.call-update) | async-done | bytes 131088 | tf_op jit(solution)/shard_map/reduce_scatter | solution.py:46
  364.9 39.0 %all-gather.9.cloned.1.call-done = bf16[256,2048]{1,0:T(8,128)(2,1)} async-done(((bf16[256,256]{1,0:T(8,128)(2,1)}), bf16[256,2048]{1,0:T(8,128)(2,1)}) %all-gather.9.cloned.1.call-update) | async-done | bytes 1048592 | tf_op jit(solution)/shard_map/all_gather | solution.py:49
  403.9 2.7 fusion.8
  406.7 17.3 %all-reduce.9.cloned.1.call-done = f32[256,256]{1,0:T(8,128)} async-done(((f32[256,256]{1,0:T(8,128)}), f32[256,256]{1,0:T(8,128)}) %all-reduce.9.cloned.1.call-update) | async-done | bytes 262160 | tf_op jit(solution)/shard_map/psum | solution.py:50
  427.7 21.7 %psum.62 = f32[256,1]{0,1:T(1,128)S(1)} all-reduce(f32[256,1]{0,1:T(1,128)S(1)} %bitcast.90), channel_id=1, replica_groups=mesh['grp'=2,'seq'=8,'mdl'=2] {'seq'}, use_global_device_ids=true, to_apply=%region_14.15 | all-reduce | flops 256 | bytes 2048 | tf_op jit(solution)/shard_map/psum | solution.py:44
  449.4 43.6 %reduce-scatter.11.cloned.1.call-done = bf16[256,256]{1,0:T(8,128)(2,1)} async-done(((bf16[256,2048]{1,0:T(8,128)(2,1)}), bf16[256,256]{1,0:T(8,128)(2,1)}) %reduce-scatter.11.cloned.1.call-update) | async-done | bytes 131088 | tf_op jit(solution)/shard_map/reduce_scatter | solution.py:46
  494.8 39.0 %all-gather.11.cloned.1.call-done = bf16[256,2048]{1,0:T(8,128)(2,1)} async-done(((bf16[256,256]{1,0:T(8,128)(2,1)}), bf16[256,2048]{1,0:T(8,128)(2,1)}) %all-gather.11.cloned.1.call-update) | async-done | bytes 1048592 | tf_op jit(solution)/shard_map/all_gather | solution.py:49
  533.8 2.7 fusion.5
  536.6 17.3 %all-reduce.11.cloned.1.call-done = f32[256,256]{1,0:T(8,128)} async-done(((f32[256,256]{1,0:T(8,128)}), f32[256,256]{1,0:T(8,128)}) %all-reduce.11.cloned.1.call-update) | async-done | bytes 262160 | tf_op jit(solution)/shard_map/psum | solution.py:50
  555.5 5.8 %all-to-all-start.1 = ((bf16[8,32,256]{2,1,0:T(8,128)(2,1)}), bf16[8,32,256]{2,1,0:T(8,128)(2,1)S(1)}, u32[]{:S(2)}, u32[]{:S(2)}) async-start(bf16[8,32,256]{2,1,0:T(8,128)(2,1)} %bitcast.27), calls=%async_computation.5 | async-start | bytes 262144 | tf_op jit(solution)/shard_map/all_to_all | solution.py:78
  561.3 7.4 %all-to-all-done.1 = bf16[8,32,256]{2,1,0:T(8,128)(2,1)S(1)} async-done(((bf16[8,32,256]{2,1,0:T(8,128)(2,1)}), bf16[8,32,256]{2,1,0:T(8,128)(2,1)S(1)}, u32[]{:S(2)}, u32[]{:S(2)}) %all-to-all-start.1) | async-done | bytes 131104 | tf_op jit(solution)/shard_map/all_to_all | solution.py:78
  (74 shorter events, 35.6 us)
Async XLA Ops:
  6.5 12.9 %copy-start = (bf16[64,128,16]{1,2,0:T(8,128)(2,1)S(1)}, bf16[64,128,16]{1,2,0:T(8,128)(2,1)}, u32[]{:S(2)}) copy-start(bf16[64,128,16]{1,2,0:T(8,128)(2,1)} %param.7) | copy-start | bytes 786436
  6.5 96.7 %reduce-scatter.5.cloned.1.call-start = ((), (), s32[]{:S(2)}) async-start(), calls=%async_computation.6 | async-start | bytes 1179648 | tf_op jit(solution)/shard_map/reduce_scatter | solution.py:46
  7.5 9.2 %collective-permute-start = (f32[4,64,128]{2,1,0:T(8,128)S(1)}, f32[4,64,128]{2,1,0:T(8,128)S(1)}, u32[]{:S(2)}, u32[]{:S(2)}) collective-permute-start(f32[4,64,128]{2,1,0:T(8,128)S(1)} %slice.49), channel_id=1, source_target_pairs={{2,0},{4,2},{6,4},{8,6},{10,8},{12,10},{14,12},{3,1},{5,3},{7,5},{... | collective-permute-start | bytes 393224 | tf_op jit(solution)/shard_map/ppermute | solution.py:14
  9.5 7.0 %copy-start.2 = (s32[4]{0:T(128)S(1)}, s32[4]{0:T(128)}, u32[]{:S(2)}) copy-start(s32[4]{0:T(128)} %param.6) | copy-start | bytes 52
  14.3 1.9 copy-start.1
  41.0 103.1 %all-gather.5.cloned.1.call-start = ((), (), s32[]{:S(2)}) async-start(), calls=%async_computation.7 | async-start | bytes 1179648 | tf_op jit(solution)/shard_map/all_gather | solution.py:49
  105.0 59.2 %all-reduce.5.cloned.1.call-start = ((), (), s32[]{:S(2)}) async-start(), calls=%async_computation.8 | async-start | bytes 524288 | tf_op jit(solution)/shard_map/psum | solution.py:50
  146.9 86.4 %reduce-scatter.7.cloned.1.call-start = ((), (), s32[]{:S(2)}) async-start(), calls=%async_computation.9 | async-start | bytes 1179648 | tf_op jit(solution)/shard_map/reduce_scatter | solution.py:46
  167.9 106.0 %all-gather.7.cloned.1.call-start = ((), (), s32[]{:S(2)}) async-start(), calls=%async_computation.10 | async-start | bytes 1179648 | tf_op jit(solution)/shard_map/all_gather | solution.py:49
  235.0 59.0 %all-reduce.7.cloned.1.call-start = ((), (), s32[]{:S(2)}) async-start(), calls=%async_computation.11 | async-start | bytes 524288 | tf_op jit(solution)/shard_map/psum | solution.py:50
  276.7 86.4 %reduce-scatter.9.cloned.1.call-start = ((), (), s32[]{:S(2)}) async-start(), calls=%async_computation.12 | async-start | bytes 1179648 | tf_op jit(solution)/shard_map/reduce_scatter | solution.py:46
  297.7 106.1 %all-gather.9.cloned.1.call-start = ((), (), s32[]{:S(2)}) async-start(), calls=%async_computation.13 | async-start | bytes 1179648 | tf_op jit(solution)/shard_map/all_gather | solution.py:49
  364.8 59.1 %all-reduce.9.cloned.1.call-start = ((), (), s32[]{:S(2)}) async-start(), calls=%async_computation.14 | async-start | bytes 524288 | tf_op jit(solution)/shard_map/psum | solution.py:50
  406.6 86.4 %reduce-scatter.11.cloned.1.call-start = ((), (), s32[]{:S(2)}) async-start(), calls=%async_computation.15 | async-start | bytes 1179648 | tf_op jit(solution)/shard_map/reduce_scatter | solution.py:46
  427.7 106.2 %all-gather.11.cloned.1.call-start = ((), (), s32[]{:S(2)}) async-start(), calls=%async_computation.16 | async-start | bytes 1179648 | tf_op jit(solution)/shard_map/all_gather | solution.py:49
  494.8 59.1 %all-reduce.11.cloned.1.call-start = ((), (), s32[]{:S(2)}) async-start(), calls=%async_computation.17 | async-start | bytes 524288 | tf_op jit(solution)/shard_map/psum | solution.py:50
  555.5 13.2 %all-to-all-start.1 = ((bf16[8,32,256]{2,1,0:T(8,128)(2,1)}), bf16[8,32,256]{2,1,0:T(8,128)(2,1)S(1)}, u32[]{:S(2)}, u32[]{:S(2)}) async-start(bf16[8,32,256]{2,1,0:T(8,128)(2,1)} %bitcast.27), calls=%async_computation.5 | async-start | bytes 262144 | tf_op jit(solution)/shard_map/all_to_all | solution.py:78
Sparse Core Ops, SparseCore 0:
  41.2 62.0 reduce-scatter.4
  105.5 38.5 all-gather.4
  147.0 17.1 all-reduce.4
  168.0 65.1 reduce-scatter.6
  235.3 38.5 all-gather.6
  276.8 17.1 all-reduce.6
  297.8 65.1 reduce-scatter.8
  365.3 38.5 all-gather.8
  406.7 17.1 all-reduce.8
  427.8 65.1 reduce-scatter.10
  495.3 38.5 all-gather.10
  536.7 17.1 all-reduce.10
where the time goes:
time: 577 us; the launch traced here: 576 us
  waiting for transfers between devices  407 us (71%)
  blocking collectives  101 us (18%)
  matrix products  27.1 us (5%)
  other arithmetic  15 us (3%)
  between operations  13.7 us (2%)
  starting transfers between devices  7.53 us (1%)
    reduce_scatter x4, waiting for transfers between devices, apply_layer(): summed = lax.psum_scatter(partial, 'seq', scatter_dimension=1, tiled=True)  174 us
    all_gather x4, waiting for transfers between devices, apply_layer(): hidden = lax.all_gather(hidden, 'seq', axis=1, tiled=True)  156 us
    psum x4, blocking collectives, apply_layer(): squares = lax.psum(jnp.sum(values * values, axis=1, keepdims=True), 'seq')  83.7 us
    psum x4, waiting for transfers between devices, apply_layer(): added = lax.psum(project_down(hidden, down_rows), 'mdl')  69.1 us
    all_to_all x1, blocking collectives, body(): state = lax.all_to_all(rows, 'seq', split_axis=1, concat_axis=0, tiled=True)  15.4 us
  transfers between devices with their start and end apart: 14, of which 13 were waited for; matrix products, arithmetic and copies ran while one was open for 1% of the time, Pallas kernels for 0%

commit v1 on v0

--- a/solution.py
+++ b/solution.py
@@ -6,6 +6,16 @@
 
 HOP = 128
 EPSILON = 1e-06
+
+
+def gather_by_hops(shard, axis, dim):
+    size = lax.axis_size(axis)
+    moving, pieces = (shard, [shard])
+    for _ in range(size - 1):
+        moving = lax.ppermute(moving, axis, [(i, (i + 1) % size) for i in range(size)])
+        pieces.insert(0, moving)
+    line = jnp.concatenate(pieces, axis=dim)
+    return jnp.roll(line, (lax.axis_index(axis) + 1) * shard.shape[dim], axis=dim)
 
 
 def shifted(x, axis, by):
@@ -46,7 +56,7 @@
     summed = lax.psum_scatter(partial, "seq", scatter_dimension=1, tiled=True)
     scale = lax.rsqrt(squares * (1.0 / width) + EPSILON)
     hidden = jax.nn.gelu(summed.astype(jnp.float32) * scale).astype(jnp.bfloat16)
-    hidden = lax.all_gather(hidden, "seq", axis=1, tiled=True)
+    hidden = gather_by_hops(hidden, "seq", 1)
     added = lax.psum(project_down(hidden, down_rows), "mdl")
     return (values + added).astype(jnp.bfloat16)
 

time: 577 us -> 633 us (1.097)
  waiting for transfers between devices: 407 us -> 461 us
    ppermute x0 -> x28, waiting for transfers between devices: none -> 216 us  [gather_by_hops(): lax.ppermute(moving, axis, [(i, (i + 1) % size) for i in range(size)])]
    all_gather x4 -> x0, waiting for transfers between devices: 156 us -> none  [apply_layer(): hidden = lax.all_gather(hidden, 'seq', axis=1, tiled=True)]
    psum x4, waiting for transfers between devices: 69.1 us -> 62.5 us  [apply_layer(): added = lax.psum(project_down(hidden, down_rows), 'mdl')]
  transfers between devices with their start and end apart: 14 -> 38, of which waited for: 13 -> 38; matrix products, arithmetic and copies ran while one was open for 1% -> 1% of each run, Pallas kernels for 0% -> 0%
where the time goes in v1:
time: 633 us; the launch traced here: 632 us
  waiting for transfers between devices  461 us (73%)
  blocking collectives  101 us (16%)
  matrix products  25.6 us (4%)
  between operations  14 us (2%)
  other arithmetic  13.3 us (2%)
  starting transfers between devices  12.5 us (2%)
    ppermute x28, waiting for transfers between devices, gather_by_hops(): lax.ppermute(moving, axis, [(i, (i + 1) % size) for i in range(size)])  216 us
    reduce_scatter x4, waiting for transfers between devices, apply_layer(): summed = lax.psum_scatter(partial, 'seq', scatter_dimension=1, tiled=True)  174 us
    psum x4, blocking collectives, apply_layer(): squares = lax.psum(jnp.sum(values * values, axis=1, keepdims=True), 'seq')  83.7 us
    psum x4, waiting for transfers between devices, apply_layer(): added = lax.psum(project_down(hidden, down_rows), 'mdl')  62.5 us
    all_to_all x1, blocking collectives, body(): state = lax.all_to_all(rows, 'seq', split_axis=1, concat_axis=0, tiled=True)  15.2 us
  transfers between devices with their start and end apart: 38, of which 38 were waited for; matrix products, arithmetic and copies ran while one was open for 1% of the time, Pallas kernels for 0%

profile of v1, /device:TPU:0, one launch (start us, length us, event | category | flops | bytes accessed | tf_op | source)
XLA Modules:
  0.0 632.4 jit_solution(7901543129248118074)
XLA Ops:
  22.1 15.2 %all_to_all.35 = bf16[32,8,256]{2,0,1:T(8,128)(2,1)S(1)} all-to-all(bf16[32,8,256]{2,0,1:T(8,128)(2,1)S(1)} %bitcast.83), channel_id=1, replica_groups=mesh['grp'=2,'seq'=8,'mdl'=2] {'seq'}, dimensions={1} | all-to-all | bytes 262144 | tf_op jit(solution)/shard_map/all_to_all | solution.py:84
  40.2 18.6 %psum.56 = f32[256,1]{0,1:T(1,128)S(1)} all-reduce(f32[256,1]{0,1:T(1,128)S(1)} %broadcast_in_dim.36), channel_id=1, replica_groups=mesh['grp'=2,'seq'=8,'mdl'=2] {'seq'}, use_global_device_ids=true, to_apply=%region_2.3 | all-reduce | flops 256 | bytes 2048 | tf_op jit(solution)/shard_map/psum | solution.py:54
  58.8 43.2 %reduce-scatter.5.cloned.1.call-done = bf16[256,256]{1,0:T(8,128)(2,1)} async-done(((bf16[256,2048]{1,0:T(8,128)(2,1)}), bf16[256,256]{1,0:T(8,128)(2,1)}) %reduce-scatter.5.cloned.1.call-update) | async-done | bytes 131088 | tf_op jit(solution)/shard_map/reduce_scatter | solution.py:56
  110.9 7.7 %collective-permute-done.2 = bf16[256,256]{1,0:T(8,128)(2,1)S(1)} collective-permute-done((bf16[256,256]{1,0:T(8,128)(2,1)S(1)}, bf16[256,256]{1,0:T(8,128)(2,1)S(1)}, u32[]{:S(2)}, u32[]{:S(2)}) %collective-permute-start.2) | collective-permute-done | bytes 131104 | tf_op jit(solution)/shard_map/ppermute | solution.py:15
  118.6 7.7 %collective-permute-done.3 = bf16[256,256]{1,0:T(8,128)(2,1)S(1)} collective-permute-done((bf16[256,256]{1,0:T(8,128)(2,1)S(1)}, bf16[256,256]{1,0:T(8,128)(2,1)S(1)}, u32[]{:S(2)}, u32[]{:S(2)}) %collective-permute-start.3) | collective-permute-done | bytes 131104 | tf_op jit(solution)/shard_map/ppermute | solution.py:15
  126.2 8.7 %collective-permute-done.4 = bf16[256,256]{1,0:T(8,128)(2,1)S(1)} collective-permute-done((bf16[256,256]{1,0:T(8,128)(2,1)S(1)}, bf16[256,256]{1,0:T(8,128)(2,1)S(1)}, u32[]{:S(2)}, u32[]{:S(2)}) %collective-permute-start.4) | collective-permute-done | bytes 131104 | tf_op jit(solution)/shard_map/ppermute | solution.py:15
  135.0 8.3 %collective-permute-done.5 = bf16[256,256]{1,0:T(8,128)(2,1)S(1)} collective-permute-done((bf16[256,256]{1,0:T(8,128)(2,1)S(1)}, bf16[256,256]{1,0:T(8,128)(2,1)S(1)}, u32[]{:S(2)}, u32[]{:S(2)}) %collective-permute-start.5) | collective-permute-done | bytes 131104 | tf_op jit(solution)/shard_map/ppermute | solution.py:15
  143.2 7.7 %collective-permute-done.6 = bf16[256,256]{1,0:T(8,128)(2,1)S(1)} collective-permute-done((bf16[256,256]{1,0:T(8,128)(2,1)S(1)}, bf16[256,256]{1,0:T(8,128)(2,1)S(1)}, u32[]{:S(2)}, u32[]{:S(2)}) %collective-permute-start.6) | collective-permute-done | bytes 131104 | tf_op jit(solution)/shard_map/ppermute | solution.py:15
  161.6 15.6 %all-reduce.5.cloned.1.call-done = f32[256,256]{1,0:T(8,128)} async-done(((f32[256,256]{1,0:T(8,128)}), f32[256,256]{1,0:T(8,128)}) %all-reduce.5.cloned.1.call-update) | async-done | bytes 262160 | tf_op jit(solution)/shard_map/psum | solution.py:60
  181.0 21.7 %psum.58 = f32[256,1]{0,1:T(1,128)S(1)} all-reduce(f32[256,1]{0,1:T(1,128)S(1)} %bitcast.92), channel_id=1, replica_groups=mesh['grp'=2,'seq'=8,'mdl'=2] {'seq'}, use_global_device_ids=true, to_apply=%region_6.8 | all-reduce | flops 256 | bytes 2048 | tf_op jit(solution)/shard_map/psum | solution.py:54
  202.7 43.6 %reduce-scatter.7.cloned.1.call-done = bf16[256,256]{1,0:T(8,128)(2,1)} async-done(((bf16[256,2048]{1,0:T(8,128)(2,1)}), bf16[256,256]{1,0:T(8,128)(2,1)}) %reduce-scatter.7.cloned.1.call-update) | async-done | bytes 131088 | tf_op jit(solution)/shard_map/reduce_scatter | solution.py:56
  270.5 8.8 %collective-permute-done.11 = bf16[256,256]{1,0:T(8,128)(2,1)S(1)} collective-permute-done((bf16[256,256]{1,0:T(8,128)(2,1)S(1)}, bf16[256,256]{1,0:T(8,128)(2,1)S(1)}, u32[]{:S(2)}, u32[]{:S(2)}) %collective-permute-start.11) | collective-permute-done | bytes 131104 | tf_op jit(solution)/shard_map/ppermute | solution.py:15
  279.3 8.2 %collective-permute-done.12 = bf16[256,256]{1,0:T(8,128)(2,1)S(1)} collective-permute-done((bf16[256,256]{1,0:T(8,128)(2,1)S(1)}, bf16[256,256]{1,0:T(8,128)(2,1)S(1)}, u32[]{:S(2)}, u32[]{:S(2)}) %collective-permute-start.12) | collective-permute-done | bytes 131104 | tf_op jit(solution)/shard_map/ppermute | solution.py:15
  305.9 15.6 %all-reduce.7.cloned.1.call-done = f32[256,256]{1,0:T(8,128)} async-done(((f32[256,256]{1,0:T(8,128)}), f32[256,256]{1,0:T(8,128)}) %all-reduce.7.cloned.1.call-update) | async-done | bytes 262160 | tf_op jit(solution)/shard_map/psum | solution.py:60
  325.3 21.7 %psum.60 = f32[256,1]{0,1:T(1,128)S(1)} all-reduce(f32[256,1]{0,1:T(1,128)S(1)} %bitcast.93), channel_id=1, replica_groups=mesh['grp'=2,'seq'=8,'mdl'=2] {'seq'}, use_global_device_ids=true, to_apply=%region_10.12 | all-reduce | flops 256 | bytes 2048 | tf_op jit(solution)/shard_map/psum | solution.py:54
  347.0 43.5 %reduce-scatter.9.cloned.1.call-done = bf16[256,256]{1,0:T(8,128)(2,1)} async-done(((bf16[256,2048]{1,0:T(8,128)(2,1)}), bf16[256,256]{1,0:T(8,128)(2,1)}) %reduce-scatter.9.cloned.1.call-update) | async-done | bytes 131088 | tf_op jit(solution)/shard_map/reduce_scatter | solution.py:56
  414.7 8.8 %collective-permute-done.18 = bf16[256,256]{1,0:T(8,128)(2,1)S(1)} collective-permute-done((bf16[256,256]{1,0:T(8,128)(2,1)S(1)}, bf16[256,256]{1,0:T(8,128)(2,1)S(1)}, u32[]{:S(2)}, u32[]{:S(2)}) %collective-permute-start.18) | collective-permute-done | bytes 131104 | tf_op jit(solution)/shard_map/ppermute | solution.py:15
  423.4 8.2 %collective-permute-done.19 = bf16[256,256]{1,0:T(8,128)(2,1)S(1)} collective-permute-done((bf16[256,256]{1,0:T(8,128)(2,1)S(1)}, bf16[256,256]{1,0:T(8,128)(2,1)S(1)}, u32[]{:S(2)}, u32[]{:S(2)}) %collective-permute-start.19) | collective-permute-done | bytes 131104 | tf_op jit(solution)/shard_map/ppermute | solution.py:15
  450.0 15.6 %all-reduce.9.cloned.1.call-done = f32[256,256]{1,0:T(8,128)} async-done(((f32[256,256]{1,0:T(8,128)}), f32[256,256]{1,0:T(8,128)}) %all-reduce.9.cloned.1.call-update) | async-done | bytes 262160 | tf_op jit(solution)/shard_map/psum | solution.py:60
  469.4 21.7 %psum.62 = f32[256,1]{0,1:T(1,128)S(1)} all-reduce(f32[256,1]{0,1:T(1,128)S(1)} %bitcast.94), channel_id=1, replica_groups=mesh['grp'=2,'seq'=8,'mdl'=2] {'seq'}, use_global_device_ids=true, to_apply=%region_14.16 | all-reduce | flops 256 | bytes 2048 | tf_op jit(solution)/shard_map/psum | solution.py:54
  491.1 43.6 %reduce-scatter.11.cloned.1.call-done = bf16[256,256]{1,0:T(8,128)(2,1)} async-done(((bf16[256,2048]{1,0:T(8,128)(2,1)}), bf16[256,256]{1,0:T(8,128)(2,1)}) %reduce-scatter.11.cloned.1.call-update) | async-done | bytes 131088 | tf_op jit(solution)/shard_map/reduce_scatter | solution.py:56
  558.9 8.8 %collective-permute-done.25 = bf16[256,256]{1,0:T(8,128)(2,1)S(1)} collective-permute-done((bf16[256,256]{1,0:T(8,128)(2,1)S(1)}, bf16[256,256]{1,0:T(8,128)(2,1)S(1)}, u32[]{:S(2)}, u32[]{:S(2)}) %collective-permute-start.25) | collective-permute-done | bytes 131104 | tf_op jit(solution)/shard_map/ppermute | solution.py:15
  567.7 8.2 %collective-permute-done.26 = bf16[256,256]{1,0:T(8,128)(2,1)S(1)} collective-permute-done((bf16[256,256]{1,0:T(8,128)(2,1)S(1)}, bf16[256,256]{1,0:T(8,128)(2,1)S(1)}, u32[]{:S(2)}, u32[]{:S(2)}) %collective-permute-start.26) | collective-permute-done | bytes 131104 | tf_op jit(solution)/shard_map/ppermute | solution.py:15
  594.2 15.7 %all-reduce.11.cloned.1.call-done = f32[256,256]{1,0:T(8,128)} async-done(((f32[256,256]{1,0:T(8,128)}), f32[256,256]{1,0:T(8,128)}) %all-reduce.11.cloned.1.call-update) | async-done | bytes 262160 | tf_op jit(solution)/shard_map/psum | solution.py:60
  (160 shorter events, 192.2 us)
Async XLA Ops:
  6.5 95.5 %reduce-scatter.5.cloned.1.call-start = ((), (), s32[]{:S(2)}) async-start(), calls=%async_computation.6 | async-start | bytes 1179648 | tf_op jit(solution)/shard_map/reduce_scatter | solution.py:56
  7.6 8.4 %collective-permute-start = (f32[4,64,128]{2,1,0:T(8,128)S(1)}, f32[4,64,128]{2,1,0:T(8,128)S(1)}, u32[]{:S(2)}, u32[]{:S(2)}) collective-permute-start(f32[4,64,128]{2,1,0:T(8,128)S(1)} %slice.49), channel_id=1, source_target_pairs={{2,0},{4,2},{6,4},{8,6},{10,8},{12,10},{14,12},{3,1},{5,3},{7,5},{... | collective-permute-start | bytes 393224 | tf_op jit(solution)/shard_map/ppermute | solution.py:24
  40.0 137.2 %all-reduce.5.cloned.1.call-start = ((), (), s32[]{:S(2)}) async-start(), calls=%async_computation.7 | async-start | bytes 524288 | tf_op jit(solution)/shard_map/psum | solution.py:60
  103.2 7.7 %collective-permute-start.1 = (bf16[256,256]{1,0:T(8,128)(2,1)S(1)}, bf16[256,256]{1,0:T(8,128)(2,1)S(1)}, u32[]{:S(2)}, u32[]{:S(2)}) collective-permute-start(bf16[256,256]{1,0:T(8,128)(2,1)S(1)} %fusion.47), channel_id=1, source_target_pairs={{0,2},{2,4},{4,6},{6,8},{8,10},{10,12},{12,14},{14,0},{1,3},{3,5},... | collective-permute-start | bytes 393224 | tf_op jit(solution)/shard_map/ppermute | solution.py:15
  110.9 7.7 %collective-permute-start.2 = (bf16[256,256]{1,0:T(8,128)(2,1)S(1)}, bf16[256,256]{1,0:T(8,128)(2,1)S(1)}, u32[]{:S(2)}, u32[]{:S(2)}) collective-permute-start(bf16[256,256]{1,0:T(8,128)(2,1)S(1)} %collective-permute-done.1), channel_id=1, source_target_pairs={{0,2},{2,4},{4,6},{6,8},{8,10},{10,12},{12,14},{14,0},{1,3},{3,5},... | collective-permute-start | bytes 393224 | tf_op jit(solution)/shard_map/ppermute | solution.py:15
  126.2 8.7 %collective-permute-start.4 = (bf16[256,256]{1,0:T(8,128)(2,1)S(1)}, bf16[256,256]{1,0:T(8,128)(2,1)S(1)}, u32[]{:S(2)}, u32[]{:S(2)}) collective-permute-start(bf16[256,256]{1,0:T(8,128)(2,1)S(1)} %collective-permute-done.3), channel_id=1, source_target_pairs={{0,2},{2,4},{4,6},{6,8},{8,10},{10,12},{12,14},{14,0},{1,3},{3,5},... | collective-permute-start | bytes 393224 | tf_op jit(solution)/shard_map/ppermute | solution.py:15
  134.9 8.3 %collective-permute-start.5 = (bf16[256,256]{1,0:T(8,128)(2,1)S(1)}, bf16[256,256]{1,0:T(8,128)(2,1)S(1)}, u32[]{:S(2)}, u32[]{:S(2)}) collective-permute-start(bf16[256,256]{1,0:T(8,128)(2,1)S(1)} %collective-permute-done.4), channel_id=1, source_target_pairs={{0,2},{2,4},{4,6},{6,8},{8,10},{10,12},{12,14},{14,0},{1,3},{3,5},... | collective-permute-start | bytes 393224 | tf_op jit(solution)/shard_map/ppermute | solution.py:15
  161.5 84.8 %reduce-scatter.7.cloned.1.call-start = ((), (), s32[]{:S(2)}) async-start(), calls=%async_computation.8 | async-start | bytes 1179648 | tf_op jit(solution)/shard_map/reduce_scatter | solution.py:56
  181.0 140.5 %all-reduce.7.cloned.1.call-start = ((), (), s32[]{:S(2)}) async-start(), calls=%async_computation.9 | async-start | bytes 524288 | tf_op jit(solution)/shard_map/psum | solution.py:60
  247.5 7.7 %collective-permute-start.8 = (bf16[256,256]{1,0:T(8,128)(2,1)S(1)}, bf16[256,256]{1,0:T(8,128)(2,1)S(1)}, u32[]{:S(2)}, u32[]{:S(2)}) collective-permute-start(bf16[256,256]{1,0:T(8,128)(2,1)S(1)} %fusion.55), channel_id=1, source_target_pairs={{0,2},{2,4},{4,6},{6,8},{8,10},{10,12},{12,14},{14,0},{1,3},{3,5},... | collective-permute-start | bytes 393224 | tf_op jit(solution)/shard_map/ppermute | solution.py:15
  270.5 8.8 %collective-permute-start.11 = (bf16[256,256]{1,0:T(8,128)(2,1)S(1)}, bf16[256,256]{1,0:T(8,128)(2,1)S(1)}, u32[]{:S(2)}, u32[]{:S(2)}) collective-permute-start(bf16[256,256]{1,0:T(8,128)(2,1)S(1)} %collective-permute-done.10), channel_id=1, source_target_pairs={{0,2},{2,4},{4,6},{6,8},{8,10},{10,12},{12,14},{14,0},{1,3},{3,5},... | collective-permute-start | bytes 393224 | tf_op jit(solution)/shard_map/ppermute | solution.py:15
  279.3 8.2 %collective-permute-start.12 = (bf16[256,256]{1,0:T(8,128)(2,1)S(1)}, bf16[256,256]{1,0:T(8,128)(2,1)S(1)}, u32[]{:S(2)}, u32[]{:S(2)}) collective-permute-start(bf16[256,256]{1,0:T(8,128)(2,1)S(1)} %collective-permute-done.11), channel_id=1, source_target_pairs={{0,2},{2,4},{4,6},{6,8},{8,10},{10,12},{12,14},{14,0},{1,3},{3,5},... | collective-permute-start | bytes 393224 | tf_op jit(solution)/shard_map/ppermute | solution.py:15
  295.2 7.7 %collective-permute-start.14 = (bf16[256,256]{1,0:T(8,128)(2,1)S(1)}, bf16[256,256]{1,0:T(8,128)(2,1)S(1)}, u32[]{:S(2)}, u32[]{:S(2)}) collective-permute-start(bf16[256,256]{1,0:T(8,128)(2,1)S(1)} %collective-permute-done.13), channel_id=1, source_target_pairs={{0,2},{2,4},{4,6},{6,8},{8,10},{10,12},{12,14},{14,0},{1,3},{3,5},... | collective-permute-start | bytes 393224 | tf_op jit(solution)/shard_map/ppermute | solution.py:15
  305.8 84.6 %reduce-scatter.9.cloned.1.call-start = ((), (), s32[]{:S(2)}) async-start(), calls=%async_computation.10 | async-start | bytes 1179648 | tf_op jit(solution)/shard_map/reduce_scatter | solution.py:56
  325.2 140.4 %all-reduce.9.cloned.1.call-start = ((), (), s32[]{:S(2)}) async-start(), calls=%async_computation.11 | async-start | bytes 524288 | tf_op jit(solution)/shard_map/psum | solution.py:60
  391.6 7.7 %collective-permute-start.15 = (bf16[256,256]{1,0:T(8,128)(2,1)S(1)}, bf16[256,256]{1,0:T(8,128)(2,1)S(1)}, u32[]{:S(2)}, u32[]{:S(2)}) collective-permute-start(bf16[256,256]{1,0:T(8,128)(2,1)S(1)} %fusion.63), channel_id=1, source_target_pairs={{0,2},{2,4},{4,6},{6,8},{8,10},{10,12},{12,14},{14,0},{1,3},{3,5},... | collective-permute-start | bytes 393224 | tf_op jit(solution)/shard_map/ppermute | solution.py:15
  414.7 8.8 %collective-permute-start.18 = (bf16[256,256]{1,0:T(8,128)(2,1)S(1)}, bf16[256,256]{1,0:T(8,128)(2,1)S(1)}, u32[]{:S(2)}, u32[]{:S(2)}) collective-permute-start(bf16[256,256]{1,0:T(8,128)(2,1)S(1)} %collective-permute-done.17), channel_id=1, source_target_pairs={{0,2},{2,4},{4,6},{6,8},{8,10},{10,12},{12,14},{14,0},{1,3},{3,5},... | collective-permute-start | bytes 393224 | tf_op jit(solution)/shard_map/ppermute | solution.py:15
  423.4 8.2 %collective-permute-start.19 = (bf16[256,256]{1,0:T(8,128)(2,1)S(1)}, bf16[256,256]{1,0:T(8,128)(2,1)S(1)}, u32[]{:S(2)}, u32[]{:S(2)}) collective-permute-start(bf16[256,256]{1,0:T(8,128)(2,1)S(1)} %collective-permute-done.18), channel_id=1, source_target_pairs={{0,2},{2,4},{4,6},{6,8},{8,10},{10,12},{12,14},{14,0},{1,3},{3,5},... | collective-permute-start | bytes 393224 | tf_op jit(solution)/shard_map/ppermute | solution.py:15
  450.0 84.7 %reduce-scatter.11.cloned.1.call-start = ((), (), s32[]{:S(2)}) async-start(), calls=%async_computation.12 | async-start | bytes 1179648 | tf_op jit(solution)/shard_map/reduce_scatter | solution.py:56
  469.4 140.5 %all-reduce.11.cloned.1.call-start = ((), (), s32[]{:S(2)}) async-start(), calls=%async_computation.13 | async-start | bytes 524288 | tf_op jit(solution)/shard_map/psum | solution.py:60
  535.9 7.7 %collective-permute-start.22 = (bf16[256,256]{1,0:T(8,128)(2,1)S(1)}, bf16[256,256]{1,0:T(8,128)(2,1)S(1)}, u32[]{:S(2)}, u32[]{:S(2)}) collective-permute-start(bf16[256,256]{1,0:T(8,128)(2,1)S(1)} %fusion.71), channel_id=1, source_target_pairs={{0,2},{2,4},{4,6},{6,8},{8,10},{10,12},{12,14},{14,0},{1,3},{3,5},... | collective-permute-start | bytes 393224 | tf_op jit(solution)/shard_map/ppermute | solution.py:15
  558.9 8.8 %collective-permute-start.25 = (bf16[256,256]{1,0:T(8,128)(2,1)S(1)}, bf16[256,256]{1,0:T(8,128)(2,1)S(1)}, u32[]{:S(2)}, u32[]{:S(2)}) collective-permute-start(bf16[256,256]{1,0:T(8,128)(2,1)S(1)} %collective-permute-done.24), channel_id=1, source_target_pairs={{0,2},{2,4},{4,6},{6,8},{8,10},{10,12},{12,14},{14,0},{1,3},{3,5},... | collective-permute-start | bytes 393224 | tf_op jit(solution)/shard_map/ppermute | solution.py:15
  567.7 8.2 %collective-permute-start.26 = (bf16[256,256]{1,0:T(8,128)(2,1)S(1)}, bf16[256,256]{1,0:T(8,128)(2,1)S(1)}, u32[]{:S(2)}, u32[]{:S(2)}) collective-permute-start(bf16[256,256]{1,0:T(8,128)(2,1)S(1)} %collective-permute-done.25), channel_id=1, source_target_pairs={{0,2},{2,4},{4,6},{6,8},{8,10},{10,12},{12,14},{14,0},{1,3},{3,5},... | collective-permute-start | bytes 393224 | tf_op jit(solution)/shard_map/ppermute | solution.py:15
  611.5 13.2 %all-to-all-start.1 = ((bf16[8,32,256]{2,1,0:T(8,128)(2,1)}), bf16[8,32,256]{2,1,0:T(8,128)(2,1)S(1)}, u32[]{:S(2)}, u32[]{:S(2)}) async-start(bf16[8,32,256]{2,1,0:T(8,128)(2,1)} %bitcast.27), calls=%async_computation.5 | async-start | bytes 262144 | tf_op jit(solution)/shard_map/all_to_all | solution.py:88
  (22 other events, 353.3 us)
Sparse Core Ops, SparseCore 0:
  40.1 61.8 reduce-scatter.4
  161.7 15.5 all-reduce.4
  181.1 65.1 reduce-scatter.6
  305.9 15.4 all-reduce.6
  325.3 65.0 reduce-scatter.8
  450.1 15.4 all-reduce.8
  469.5 65.1 reduce-scatter.10
  594.3 15.4 all-reduce.10
